TPU v7x, 256 devices: a whole 4x4x8 slice. The times are simulated.
256 devices in a mesh: cell: 64 (over y, z, core), view: 4 (over x).
Axes of the slice: x: 4, y: 4, z: 8, core: 2. Of those that a mesh axis runs over, the one named last changes fastest.
Arguments:
- gaussians: float32 [1024, 9, 256], P('cell'), as said below
- seg_count: int32 [4, 64], P('view', 'cell'), may hold values from 1 to 3, as said below
- seg_block: int32 [4, 64, 3], P('view', 'cell'), may hold values from 0 to 1023, as said below
- ray_count: int32 [4, 64], P('view', 'cell'), may hold values from 576 to 2304
- camera_shift: float32 [4, 2], P('view'), may hold values from -6 to 6
- target: float32 [4, 64, 3, 2304], P('view', 'cell'), may hold values from 0 to 1
Outputs:
- image: float32 [4, 64, 3, 2304], P('view', 'cell')
- gauss_grad: float32 [1024, 9, 256], P('cell')
Inputs may be any that keep to these rules, and one draw needn't show every extreme that they name: `gaussians`: each column of a block is one Gaussian: a mean, the entries a, b, c of a positive definite inverse covariance, an opacity in (0, 1), three colours. `seg_count`: tiles 2m and 2m + 1 of a view hold 4 segments together; in every view some tile holds 3. Segment k of tile t uses a block stored in cell seg_block // 16, which is t + e modulo 64 for some e from -2 to 2; entries at k >= seg_count are not used.
All inputs are finite; a program needn't handle non-finite values.
Results may differ from a plain program's by a relative error of at most 0.0003.
Values sent between devices are 32-bit elements; how exact they have to be, the bound alone decides.
No kernel may reach another device: no remote copies, remote signals or barrier semaphores. Data moves between devices by JAX's collectives and lax.ppermute only.
A program may use at most 64 MiB of HBM per device.

v0:
```python
import jax
import jax.numpy as jnp
from jax import lax
from jax.sharding import PartitionSpec as P

TILE = 48
REACH = 2
precise = lax.Precision.HIGHEST


def shifted(block, axis, distance):
    devices = range(lax.axis_size(axis))
    route = [((i - distance) % len(devices), i) for i in devices]
    return lax.ppermute(block, axis, route)


def pixel_frame(shift, pixels):
    pixel_ids = jnp.arange(pixels)
    centre = (TILE - 1) / 2.0
    pix_x = (pixel_ids % TILE).astype(jnp.float32) - centre - shift[0]
    pix_y = (pixel_ids // TILE).astype(jnp.float32) - centre - shift[1]
    return (pix_x, pix_y)


def triangles(length):
    row_ids = lax.broadcasted_iota(jnp.int32, (length, length), 0)
    col_ids = lax.broadcasted_iota(jnp.int32, (length, length), 1)
    return ((col_ids < row_ids).astype(jnp.float32), (col_ids > row_ids).astype(jnp.float32))


def splat(params, pix_x, pix_y):
    delta_x = pix_x[None, :] - params[0][:, None]
    delta_y = pix_y[None, :] - params[1][:, None]
    quad_form = (
        params[2][:, None] * delta_x * delta_x
        + 2.0 * params[3][:, None] * delta_x * delta_y
        + params[4][:, None] * delta_y * delta_y
    )
    alphas = params[5][:, None] * jnp.exp(-0.5 * quad_form)
    return (alphas, jnp.log1p(-alphas))


def forward_task(params, pix_x, pix_y, lower_tri):
    alphas, log_trans = splat(params, pix_x, pix_y)
    prefix = jnp.dot(lower_tri, log_trans, precision=precise, preferred_element_type=jnp.float32)
    weights = alphas * jnp.exp(prefix)
    colour = jnp.dot(params[6:9], weights, precision=precise, preferred_element_type=jnp.float32)
    totals = jnp.sum(log_trans, axis=0)
    return jnp.concatenate([colour, totals[None, :]], axis=0)


def gradient_rows(params, pix_x, pix_y, weighted, weights, weight_cot):
    features = jnp.stack(
        [jnp.ones_like(pix_x), pix_x, pix_y, pix_x * pix_x, pix_x * pix_y, pix_y * pix_y]
    )
    moments = lax.dot_general(
        features,
        weighted,
        (((1,), (1,)), ((), ())),
        precision=precise,
        preferred_element_type=jnp.float32,
    )
    colour_grad = lax.dot_general(
        weight_cot,
        weights,
        (((1,), (1,)), ((), ())),
        precision=precise,
        preferred_element_type=jnp.float32,
    )
    mean_x, mean_y, conic_a, conic_b, conic_c, opacity = (
        params[0],
        params[1],
        params[2],
        params[3],
        params[4],
        params[5],
    )
    moment_zero = moments[0]
    along_x = moments[1] - mean_x * moment_zero
    along_y = moments[2] - mean_y * moment_zero
    square_x = moments[3] - 2.0 * mean_x * moments[1] + mean_x * mean_x * moment_zero
    cross_xy = (
        moments[4] - mean_x * moments[2] - mean_y * moments[1] + mean_x * mean_y * moment_zero
    )
    square_y = moments[5] - 2.0 * mean_y * moments[2] + mean_y * mean_y * moment_zero
    grad_rows = jnp.stack(
        [
            conic_a * along_x + conic_b * along_y,
            conic_b * along_x + conic_c * along_y,
            -0.5 * square_x,
            -cross_xy,
            -0.5 * square_y,
            moment_zero / opacity,
        ]
    )
    return jnp.concatenate([grad_rows, colour_grad], axis=0)


def backward_task(params, cotangent, pix_x, pix_y, lower_tri, upper_tri):
    alphas, log_trans = splat(params, pix_x, pix_y)
    transmit = jnp.exp(
        jnp.dot(lower_tri, log_trans, precision=precise, preferred_element_type=jnp.float32)
    )
    weights = alphas * transmit
    weight_cot = cotangent[:3]
    shaded = lax.dot_general(
        params[6:9],
        weight_cot,
        (((0,), (0,)), ((), ())),
        precision=precise,
        preferred_element_type=jnp.float32,
    )
    later_sum = jnp.dot(
        upper_tri, weights * shaded, precision=precise, preferred_element_type=jnp.float32
    )
    dalpha = transmit * shaded - (later_sum + cotangent[3][None, :]) / (1.0 - alphas)
    return gradient_rows(params, pix_x, pix_y, dalpha * alphas, weights, weight_cot)


def composite(partials, live_mask, target_tile, valid_slot):
    slot_total = partials.shape[0]
    running = jnp.zeros(partials.shape[2:], jnp.float32)
    transmit = []
    for slot_index in range(slot_total):
        transmit.append(jnp.exp(running))
        running = running + partials[slot_index, 3]
    transmit = jnp.stack(transmit)
    shaded = transmit[:, None, :] * partials[:, :3]
    rendered = jnp.sum(shaded, axis=0) * live_mask
    residual = (rendered - target_tile) * live_mask
    behind = []
    running_sum = jnp.zeros_like(rendered)
    for slot_index in range(slot_total - 1, -1, -1):
        behind.insert(0, running_sum)
        running_sum = running_sum + shaded[slot_index]
    behind = jnp.stack(behind)
    valid_weight = valid_slot.astype(jnp.float32)
    weight_cot = transmit[:, None, :] * residual[None] * valid_weight[:, None, None]
    after_cot = jnp.sum(residual[None] * behind, axis=1) * valid_weight[:, None]
    return (rendered, jnp.concatenate([weight_cot, after_cot[:, None, :]], axis=1))


def shards(gaussians, seg_count, seg_block, ray_count, camera_shift, target):
    cell_count = lax.axis_size("cell")
    cell_index = lax.axis_index("cell")
    per_block = gaussians.shape[0]
    pixels = target.shape[3]
    lower_tri, upper_tri = triangles(gaussians.shape[2])
    blocks = seg_block[0, 0]
    slot_count = blocks.shape[0]
    own_count = seg_count[0, 0]
    home_cell = blocks // per_block
    local_block = blocks % per_block
    offset = (home_cell - cell_index + REACH) % cell_count - REACH
    pix_x, pix_y = pixel_frame(camera_shift[0], pixels)
    valid_slot = jnp.arange(slot_count) < own_count

    def run_forward(params):
        return forward_task(params, pix_x, pix_y, lower_tri)

    def run_backward(bundle):
        return backward_task(bundle[0], bundle[1], pix_x, pix_y, lower_tri, upper_tri)

    near_list = []
    for shift_by in range(-REACH, REACH + 1):
        if shift_by == 0:
            near_list.append(gaussians)
        else:
            near_list.append(shifted(gaussians, "cell", -shift_by))
    near_stack = jnp.concatenate(near_list, axis=0)
    pick_index = (offset + REACH) * per_block + local_block
    own_params = jnp.take(near_stack, pick_index, axis=0)
    partials = lax.map(run_forward, own_params)
    partials = jnp.where(valid_slot[:, None, None], partials, 0.0)
    live_mask = (jnp.arange(pixels) < ray_count[0, 0]).astype(jnp.float32)
    rendered, cotangent = composite(partials, live_mask, target[0, 0], valid_slot)
    own_grads = lax.map(run_backward, (own_params, cotangent))
    spot_count = (2 * REACH + 1) * per_block
    onehot = (pick_index[:, None] == jnp.arange(spot_count)[None, :]).astype(jnp.float32)
    spread = jnp.einsum("sk,sjg->kjg", onehot, own_grads, precision=precise)
    spread = spread.reshape((2 * REACH + 1, per_block) + gaussians.shape[1:])
    block_grads = spread[REACH]
    for shift_by in range(-REACH, REACH + 1):
        if shift_by != 0:
            block_grads = block_grads + shifted(spread[shift_by + REACH], "cell", shift_by)
    gauss_grad = lax.psum(block_grads, "view")
    return (rendered[None, None], gauss_grad)


def solution(mesh):
    placed = (
        P("cell", None, None),
        P("view", "cell"),
        P("view", "cell", None),
        P("view", "cell"),
        P("view", None),
        P("view", "cell", None, None),
    )
    return jax.shard_map(
        shards,
        mesh=mesh,
        in_specs=placed,
        out_specs=(P("view", "cell", None, None), P("cell", None, None)),
        check_vma=False,
    )
```

profile of v0, /device:TPU:8, one launch (start us, length us, event | category | flops | bytes accessed | tf_op | source)
XLA Modules:
  0.0 183.9 jit_solution(16609155894614825310)
XLA Ops:
  7.2 1.0 copy.22
  8.2 2.0 %collective-permute-start = (f32[16,9,256]{2,1,0:T(8,128)S(1)}, f32[16,9,256]{2,1,0:T(8,128)S(1)}, u32[]{:S(2)}, u32[]{:S(2)}) collective-permute-start(f32[16,9,256]{2,1,0:T(8,128)S(1)} %copy.22), channel_id=1, source_target_pairs={{248,0},{252,4},{0,8},{4,12},{8,16},{12,20},{16,24},{20,28},{24,32... | collective-permute-start | bytes 442376 | tf_op jit(solution)/shard_map/ppermute | solution.py:14
  10.2 3.9 %collective-permute-start.2 = (f32[16,9,256]{2,1,0:T(8,128)S(1)}, f32[16,9,256]{2,1,0:T(8,128)S(1)}, u32[]{:S(2)}, u32[]{:S(2)}) collective-permute-start(f32[16,9,256]{2,1,0:T(8,128)S(1)} %copy.22), channel_id=1, source_target_pairs={{4,0},{8,4},{12,8},{16,12},{20,16},{24,20},{28,24},{32,28},{36,32}... | collective-permute-start | bytes 442376 | tf_op jit(solution)/shard_map/ppermute | solution.py:14
  14.1 1.8 collective-permute-start.3
  15.9 0.7 fusion.126
  16.5 0.7 compare_and_fusion
  17.2 1.4 fusion.131
  20.1 1.1 collective-permute-done
  21.2 0.7 constant_dynamic-update-slice_fusion.3
  21.9 1.2 collective-permute-done.1
  23.1 0.7 constant_dynamic-update-slice_fusion.2
  23.9 1.7 copy_dynamic-update-slice_fusion
  25.6 0.7 constant_dynamic-update-slice_fusion.1
  26.3 0.7 constant_dynamic-update-slice_fusion
  27.0 1.9 %gather_fusion = f32[3,9,256]{2,1,0:T(8,128)S(1)} fusion(f32[80,9,256]{2,1,0:T(8,128)} %constant_dynamic-update-slice_fusion, s32[1024]{0:T(1024)S(1)} %pad_clamp_fusion), kind=kCustom, calls=%fused_computation | custom fusion | bytes 55308 | tf_op jit(solution)/shard_map/jit(_take)/gather | solution.py:172
  29.0 30.8 %while.26 = (s32[]{:T(128)}, f32[3,4,2304]{2,1,0:T(4,128)S(1)}, f32[3,9,256]{2,1,0:T(8,128)S(1)}, f32[]{:T(128)}, f32[]{:T(128)}) while((s32[]{:T(128)}, f32[3,4,2304]{2,1,0:T(4,128)S(1)}, f32[3,9,256]{2,1,0:T(8,128)S(1)}, f32[]{:T(128)}, f32[]{:T(128)}) %tuple.102), condition=%wide.region_2.3_spmd.clone.clone, body=%wide.region_0.2_spmd.clone.sunk.clone | while | flops 1856945664 | bytes 4940977 | solution.py:173
  29.0 1.2 fusion.185
  30.2 4.6 %fusion.187 = f32[256,2304]{0,1:T(8,128)S(1)} fusion(f32[256]{0:T(256)S(1)} %bitcast.284, f32[256]{0:T(256)S(1)} %bitcast.276, f32[2304]{0:T(1024)S(1)} %get-tuple-element.382, f32[256]{0:T(256)S(1)} %bitcast.278, f32[256]{0:T(256)S(1)} %bitcast.280, f32[2304]{0:T(1024)S(1)} %get-tuple-element.385, f32[256]{0:T(256)S(1)} %bitcast.282, ...), kind=kOutput, calls=%fused_computation.19.clone.1.clone | convolution fusion | flops 1827405824 | bytes 2383872 | tf_op jit(solution)/shard_map/while/body/eval_jaxpr/dot_general | solution.py:45
  34.9 2.0 %fusion.188 = f32[3,2304]{1,0:T(4,128)S(1)} fusion(f32[256,2304]{0,1:T(8,128)S(1)} %fusion.187, f32[3,9,256]{2,1,0:T(8,128)S(1)} %get-tuple-element.451, s32[]{:T(128)} %get-tuple-element.444, s32[]{:T(128)S(6)} %add.582), kind=kOutput, calls=%fused_computation.48.clone.1.clone | convolution fusion | flops 21233664 | bytes 2391048 | tf_op jit(solution)/shard_map/while/body/eval_jaxpr/dot_general | solution.py:47
  36.9 2.3 %fusion.186 = f32[2304]{0:T(1024)S(1)} fusion(f32[256]{0:T(256)S(1)} %bitcast.285, f32[256]{0:T(256)S(1)} %bitcast.277, f32[2304]{0:T(1024)S(1)} %get-tuple-element.382, f32[256]{0:T(256)S(1)} %bitcast.279, f32[256]{0:T(256)S(1)} %bitcast.281, f32[2304]{0:T(1024)S(1)} %get-tuple-element.385, f32[256]{0:T(256)S(1)} %bitcast.283, f32[256]{0:T(256)S(1)} %bitcast.275), kind=kLoop, calls=%fused_computation.26.clone.1.clone | loop fusion | flops 8255232 | bytes 33792 | tf_op jit(solution)/shard_map/while/body/eval_jaxpr/reduce_sum | solution.py:48
  39.3 1.2 fusion.185
  40.5 4.6 %fusion.187 = f32[256,2304]{0,1:T(8,128)S(1)} fusion(f32[256]{0:T(256)S(1)} %bitcast.284, f32[256]{0:T(256)S(1)} %bitcast.276, f32[2304]{0:T(1024)S(1)} %get-tuple-element.382, f32[256]{0:T(256)S(1)} %bitcast.278, f32[256]{0:T(256)S(1)} %bitcast.280, f32[2304]{0:T(1024)S(1)} %get-tuple-element.385, f32[256]{0:T(256)S(1)} %bitcast.282, ...), kind=kOutput, calls=%fused_computation.19.clone.1.clone | convolution fusion | flops 1827405824 | bytes 2383872 | tf_op jit(solution)/shard_map/while/body/eval_jaxpr/dot_general | solution.py:45
  45.1 2.0 %fusion.188 = f32[3,2304]{1,0:T(4,128)S(1)} fusion(f32[256,2304]{0,1:T(8,128)S(1)} %fusion.187, f32[3,9,256]{2,1,0:T(8,128)S(1)} %get-tuple-element.451, s32[]{:T(128)} %get-tuple-element.444, s32[]{:T(128)S(6)} %add.582), kind=kOutput, calls=%fused_computation.48.clone.1.clone | convolution fusion | flops 21233664 | bytes 2391048 | tf_op jit(solution)/shard_map/while/body/eval_jaxpr/dot_general | solution.py:47
  47.1 2.3 %fusion.186 = f32[2304]{0:T(1024)S(1)} fusion(f32[256]{0:T(256)S(1)} %bitcast.285, f32[256]{0:T(256)S(1)} %bitcast.277, f32[2304]{0:T(1024)S(1)} %get-tuple-element.382, f32[256]{0:T(256)S(1)} %bitcast.279, f32[256]{0:T(256)S(1)} %bitcast.281, f32[2304]{0:T(1024)S(1)} %get-tuple-element.385, f32[256]{0:T(256)S(1)} %bitcast.283, f32[256]{0:T(256)S(1)} %bitcast.275), kind=kLoop, calls=%fused_computation.26.clone.1.clone | loop fusion | flops 8255232 | bytes 33792 | tf_op jit(solution)/shard_map/while/body/eval_jaxpr/reduce_sum | solution.py:48
  49.5 1.2 fusion.185
  50.8 4.6 %fusion.187 = f32[256,2304]{0,1:T(8,128)S(1)} fusion(f32[256]{0:T(256)S(1)} %bitcast.284, f32[256]{0:T(256)S(1)} %bitcast.276, f32[2304]{0:T(1024)S(1)} %get-tuple-element.382, f32[256]{0:T(256)S(1)} %bitcast.278, f32[256]{0:T(256)S(1)} %bitcast.280, f32[2304]{0:T(1024)S(1)} %get-tuple-element.385, f32[256]{0:T(256)S(1)} %bitcast.282, ...), kind=kOutput, calls=%fused_computation.19.clone.1.clone | convolution fusion | flops 1827405824 | bytes 2383872 | tf_op jit(solution)/shard_map/while/body/eval_jaxpr/dot_general | solution.py:45
  55.4 2.0 %fusion.188 = f32[3,2304]{1,0:T(4,128)S(1)} fusion(f32[256,2304]{0,1:T(8,128)S(1)} %fusion.187, f32[3,9,256]{2,1,0:T(8,128)S(1)} %get-tuple-element.451, s32[]{:T(128)} %get-tuple-element.444, s32[]{:T(128)S(6)} %add.582), kind=kOutput, calls=%fused_computation.48.clone.1.clone | convolution fusion | flops 21233664 | bytes 2391048 | tf_op jit(solution)/shard_map/while/body/eval_jaxpr/dot_general | solution.py:47
  57.4 2.3 %fusion.186 = f32[2304]{0:T(1024)S(1)} fusion(f32[256]{0:T(256)S(1)} %bitcast.285, f32[256]{0:T(256)S(1)} %bitcast.277, f32[2304]{0:T(1024)S(1)} %get-tuple-element.382, f32[256]{0:T(256)S(1)} %bitcast.279, f32[256]{0:T(256)S(1)} %bitcast.281, f32[2304]{0:T(1024)S(1)} %get-tuple-element.385, f32[256]{0:T(256)S(1)} %bitcast.283, f32[256]{0:T(256)S(1)} %bitcast.275), kind=kLoop, calls=%fused_computation.26.clone.1.clone | loop fusion | flops 8255232 | bytes 33792 | tf_op jit(solution)/shard_map/while/body/eval_jaxpr/reduce_sum | solution.py:48
  60.4 57.0 %while.27 = (s32[]{:T(128)}, f32[3,9,256]{2,0,1:T(4,128)S(1)}, f32[3,9,256]{2,1,0:T(8,128)S(1)}, f32[3,4,2304]{2,1,0:T(4,128)S(1)}, f32[]{:T(128)}, /*index=5*/f32[]{:T(128)}) while((s32[]{:T(128)}, f32[3,9,256]{2,0,1:T(4,128)S(1)}, f32[3,9,256]{2,1,0:T(8,128)S(1)}, f32[3,4,2304]{2,1,0:T(4,128)S(1)}, ...), condition=%wide.region_6.7_spmd.clone.clone.clone, body=%wide.region_5.6_spmd.clone.clone.sunk.clone | while | flops 3743404544 | bytes 35934480 | solution.py:177
  60.6 1.2 fusion.197
  61.8 4.9 %fusion.201 = f32[256,2304]{0,1:T(8,128)} fusion(f32[256]{0:T(256)S(1)} %bitcast.265, f32[256]{0:T(256)S(1)} %bitcast.256, f32[2304]{0:T(1024)S(1)} %get-tuple-element.410, f32[256]{0:T(256)S(1)} %bitcast.271, f32[256]{0:T(256)S(1)} %bitcast.259, f32[2304]{0:T(1024)S(1)} %get-tuple-element.409, f32[256]{0:T(256)S(1)} %bitcast.268, ...), kind=kOutput, calls=%fused_computation.66.clone.1.clone | convolution fusion | flops 1819738112 | bytes 2383872 | tf_op jit(solution)/shard_map/while/body/eval_jaxpr/dot_general | solution.py:102
  66.8 2.1 %fusion.200 = f32[256,2304]{0,1:T(8,128)S(1)} fusion(f32[3,4,2304]{2,1,0:T(4,128)S(1)} %get-tuple-element.469, s32[]{:T(128)} %get-tuple-element.460, f32[3,9,256]{2,1,0:T(8,128)S(1)} %get-tuple-element.468, s32[]{:T(128)S(6)} %add.601), kind=kOutput, calls=%fused_computation.88.clone.1.clone | convolution fusion | flops 21233664 | bytes 2401284 | tf_op jit(solution)/shard_map/while/body/eval_jaxpr/dot_general | solution.py:106
  68.9 4.4 %fusion.202 = f32[256,2304]{0,1:T(8,128)S(1)} fusion(f32[256,2304]{0,1:T(8,128)S(1)} %fusion.200, f32[256,2304]{0,1:T(8,128)S(1)} %copy-done.1, f32[2304]{0:T(1024)S(1)} %dynamic-slice_reduce_fusion.3, f32[256]{0:T(256)S(1)} %bitcast.266, f32[256]{0:T(256)S(1)} %bitcast.257, f32[2304]{0:T(1024)S(1)} %get-tuple-element.410, ...), kind=kOutput, calls=%fused_computation.70.clone.1.clone | convolution fusion | flops 1830944768 | bytes 7111680 | tf_op jit(solution)/shard_map/while/body/eval_jaxpr/dot_general | solution.py:113
  73.4 1.2 fusion.199
  74.6 0.6 fusion.198
  75.4 1.0 fusion.203
  76.4 0.6 copy-done.2
  77.0 2.2 %fusion.205 = f32[3,256]{1,0:T(4,128)S(1)} fusion(f32[256,2304]{0,1:T(8,128)S(1)} %copy-done.2, f32[256]{0:T(256)S(1)} %bitcast.267, f32[256]{0:T(256)S(1)} %bitcast.258, f32[2304]{0:T(1024)S(1)} %get-tuple-element.410, f32[256]{0:T(256)S(1)} %bitcast.273, f32[256]{0:T(256)S(1)} %bitcast.261, f32[2304]{0:T(1024)S(1)} %get-tuple-element.409, ...), kind=kOutput, calls=%fused_computation.80.clone.1.clone | convolution fusion | flops 28901376 | bytes 2429956 | tf_op jit(solution)/shard_map/while/body/eval_jaxpr/dot_general | solution.py:63
  79.5 1.2 fusion.197
  80.7 4.9 %fusion.201 = f32[256,2304]{0,1:T(8,128)} fusion(f32[256]{0:T(256)S(1)} %bitcast.265, f32[256]{0:T(256)S(1)} %bitcast.256, f32[2304]{0:T(1024)S(1)} %get-tuple-element.410, f32[256]{0:T(256)S(1)} %bitcast.271, f32[256]{0:T(256)S(1)} %bitcast.259, f32[2304]{0:T(1024)S(1)} %get-tuple-element.409, f32[256]{0:T(256)S(1)} %bitcast.268, ...), kind=kOutput, calls=%fused_computation.66.clone.1.clone | convolution fusion | flops 1819738112 | bytes 2383872 | tf_op jit(solution)/shard_map/while/body/eval_jaxpr/dot_general | solution.py:102
  85.6 2.1 %fusion.200 = f32[256,2304]{0,1:T(8,128)S(1)} fusion(f32[3,4,2304]{2,1,0:T(4,128)S(1)} %get-tuple-element.469, s32[]{:T(128)} %get-tuple-element.460, f32[3,9,256]{2,1,0:T(8,128)S(1)} %get-tuple-element.468, s32[]{:T(128)S(6)} %add.601), kind=kOutput, calls=%fused_computation.88.clone.1.clone | convolution fusion | flops 21233664 | bytes 2401284 | tf_op jit(solution)/shard_map/while/body/eval_jaxpr/dot_general | solution.py:106
  87.8 4.4 %fusion.202 = f32[256,2304]{0,1:T(8,128)S(1)} fusion(f32[256,2304]{0,1:T(8,128)S(1)} %fusion.200, f32[256,2304]{0,1:T(8,128)S(1)} %copy-done.1, f32[2304]{0:T(1024)S(1)} %dynamic-slice_reduce_fusion.3, f32[256]{0:T(256)S(1)} %bitcast.266, f32[256]{0:T(256)S(1)} %bitcast.257, f32[2304]{0:T(1024)S(1)} %get-tuple-element.410, ...), kind=kOutput, calls=%fused_computation.70.clone.1.clone | convolution fusion | flops 1830944768 | bytes 7111680 | tf_op jit(solution)/shard_map/while/body/eval_jaxpr/dot_general | solution.py:113
  92.2 1.2 fusion.199
  93.5 0.6 fusion.198
  94.2 1.0 fusion.203
  95.3 0.6 copy-done.2
  95.9 2.2 %fusion.205 = f32[3,256]{1,0:T(4,128)S(1)} fusion(f32[256,2304]{0,1:T(8,128)S(1)} %copy-done.2, f32[256]{0:T(256)S(1)} %bitcast.267, f32[256]{0:T(256)S(1)} %bitcast.258, f32[2304]{0:T(1024)S(1)} %get-tuple-element.410, f32[256]{0:T(256)S(1)} %bitcast.273, f32[256]{0:T(256)S(1)} %bitcast.261, f32[2304]{0:T(1024)S(1)} %get-tuple-element.409, ...), kind=kOutput, calls=%fused_computation.80.clone.1.clone | convolution fusion | flops 28901376 | bytes 2429956 | tf_op jit(solution)/shard_map/while/body/eval_jaxpr/dot_general | solution.py:63
  98.4 1.2 fusion.197
  99.6 4.9 %fusion.201 = f32[256,2304]{0,1:T(8,128)} fusion(f32[256]{0:T(256)S(1)} %bitcast.265, f32[256]{0:T(256)S(1)} %bitcast.256, f32[2304]{0:T(1024)S(1)} %get-tuple-element.410, f32[256]{0:T(256)S(1)} %bitcast.271, f32[256]{0:T(256)S(1)} %bitcast.259, f32[2304]{0:T(1024)S(1)} %get-tuple-element.409, f32[256]{0:T(256)S(1)} %bitcast.268, ...), kind=kOutput, calls=%fused_computation.66.clone.1.clone | convolution fusion | flops 1819738112 | bytes 2383872 | tf_op jit(solution)/shard_map/while/body/eval_jaxpr/dot_general | solution.py:102
  104.5 2.1 %fusion.200 = f32[256,2304]{0,1:T(8,128)S(1)} fusion(f32[3,4,2304]{2,1,0:T(4,128)S(1)} %get-tuple-element.469, s32[]{:T(128)} %get-tuple-element.460, f32[3,9,256]{2,1,0:T(8,128)S(1)} %get-tuple-element.468, s32[]{:T(128)S(6)} %add.601), kind=kOutput, calls=%fused_computation.88.clone.1.clone | convolution fusion | flops 21233664 | bytes 2401284 | tf_op jit(solution)/shard_map/while/body/eval_jaxpr/dot_general | solution.py:106
  106.7 4.4 %fusion.202 = f32[256,2304]{0,1:T(8,128)S(1)} fusion(f32[256,2304]{0,1:T(8,128)S(1)} %fusion.200, f32[256,2304]{0,1:T(8,128)S(1)} %copy-done.1, f32[2304]{0:T(1024)S(1)} %dynamic-slice_reduce_fusion.3, f32[256]{0:T(256)S(1)} %bitcast.266, f32[256]{0:T(256)S(1)} %bitcast.257, f32[2304]{0:T(1024)S(1)} %get-tuple-element.410, ...), kind=kOutput, calls=%fused_computation.70.clone.1.clone | convolution fusion | flops 1830944768 | bytes 7111680 | tf_op jit(solution)/shard_map/while/body/eval_jaxpr/dot_general | solution.py:113
  111.1 1.2 fusion.199
  112.4 0.6 fusion.198
  113.1 1.0 fusion.203
  114.7 2.2 %fusion.205 = f32[3,256]{1,0:T(4,128)S(1)} fusion(f32[256,2304]{0,1:T(8,128)S(1)} %copy-done.2, f32[256]{0:T(256)S(1)} %bitcast.267, f32[256]{0:T(256)S(1)} %bitcast.258, f32[2304]{0:T(1024)S(1)} %get-tuple-element.410, f32[256]{0:T(256)S(1)} %bitcast.273, f32[256]{0:T(256)S(1)} %bitcast.261, f32[2304]{0:T(1024)S(1)} %get-tuple-element.409, ...), kind=kOutput, calls=%fused_computation.80.clone.1.clone | convolution fusion | flops 28901376 | bytes 2429956 | tf_op jit(solution)/shard_map/while/body/eval_jaxpr/dot_general | solution.py:63
  118.0 1.8 collective-permute-start.4
  120.6 2.6 %collective-permute-done.4 = f32[16,9,256]{2,0,1:T(8,128)S(1)} collective-permute-done((f32[16,9,256]{2,0,1:T(8,128)S(1)}, f32[16,9,256]{2,0,1:T(8,128)S(1)}, u32[]{:S(2)}, u32[]{:S(2)}) %collective-permute-start.4) | collective-permute-done | bytes 147488 | tf_op jit(solution)/shard_map/ppermute | solution.py:14
  123.2 0.8 collective-permute-done.5
  124.1 2.9 %collective-permute-done.6 = f32[16,9,256]{2,0,1:T(8,128)S(1)} collective-permute-done((f32[16,9,256]{2,0,1:T(8,128)S(1)}, f32[16,9,256]{2,0,1:T(8,128)S(1)}, u32[]{:S(2)}, u32[]{:S(2)}) %collective-permute-start.6) | collective-permute-done | bytes 147488 | tf_op jit(solution)/shard_map/ppermute | solution.py:14
  127.0 2.2 %collective-permute-done.7 = f32[16,9,256]{2,0,1:T(8,128)S(1)} collective-permute-done((f32[16,9,256]{2,0,1:T(8,128)S(1)}, f32[16,9,256]{2,0,1:T(8,128)S(1)}, u32[]{:S(2)}, u32[]{:S(2)}) %collective-permute-start.7) | collective-permute-done | bytes 147488 | tf_op jit(solution)/shard_map/ppermute | solution.py:14
  129.2 0.7 fusion.110
  129.9 0.6 reshape_multiply_fusion.1
  130.5 44.9 %all-reduce.2.cloned.1.call-done = f32[16,9,256]{2,0,1:T(8,128)} async-done(((f32[16,9,256]{2,0,1:T(8,128)}), f32[16,9,256]{2,0,1:T(8,128)}) %all-reduce.2.cloned.1.call-update) | async-done | bytes 147472 | tf_op jit(solution)/shard_map/psum | solution.py:186
  175.5 1.6 copy.63
  (81 shorter events, 4.3 us)
Async XLA Ops:
  7.2 168.3 %all-reduce.2.cloned.1.call-start = ((), (), s32[]{:S(2)}) async-start(), calls=%async_computation | async-start | bytes 294912 | tf_op jit(solution)/shard_map/psum | solution.py:186
  8.2 13.0 %collective-permute-start = (f32[16,9,256]{2,1,0:T(8,128)S(1)}, f32[16,9,256]{2,1,0:T(8,128)S(1)}, u32[]{:S(2)}, u32[]{:S(2)}) collective-permute-start(f32[16,9,256]{2,1,0:T(8,128)S(1)} %copy.22), channel_id=1, source_target_pairs={{248,0},{252,4},{0,8},{4,12},{8,16},{12,20},{16,24},{20,28},{24,32... | collective-permute-start | bytes 442376 | tf_op jit(solution)/shard_map/ppermute | solution.py:14
  10.2 12.9 %collective-permute-start.1 = (f32[16,9,256]{2,1,0:T(8,128)S(1)}, f32[16,9,256]{2,1,0:T(8,128)S(1)}, u32[]{:S(2)}, u32[]{:S(2)}) collective-permute-start(f32[16,9,256]{2,1,0:T(8,128)S(1)} %copy.22), channel_id=1, source_target_pairs={{252,0},{0,4},{4,8},{8,12},{12,16},{16,20},{20,24},{24,28},{28,32}... | collective-permute-start | bytes 442376 | tf_op jit(solution)/shard_map/ppermute | solution.py:14
  10.2 15.4 %collective-permute-start.2 = (f32[16,9,256]{2,1,0:T(8,128)S(1)}, f32[16,9,256]{2,1,0:T(8,128)S(1)}, u32[]{:S(2)}, u32[]{:S(2)}) collective-permute-start(f32[16,9,256]{2,1,0:T(8,128)S(1)} %copy.22), channel_id=1, source_target_pairs={{4,0},{8,4},{12,8},{16,12},{20,16},{24,20},{28,24},{32,28},{36,32}... | collective-permute-start | bytes 442376 | tf_op jit(solution)/shard_map/ppermute | solution.py:14
  14.1 12.2 %collective-permute-start.3 = (f32[16,9,256]{2,1,0:T(8,128)S(1)}, f32[16,9,256]{2,1,0:T(8,128)S(1)}, u32[]{:S(2)}, u32[]{:S(2)}) collective-permute-start(f32[16,9,256]{2,1,0:T(8,128)S(1)} %copy.22), channel_id=1, source_target_pairs={{8,0},{12,4},{16,8},{20,12},{24,16},{28,20},{32,24},{36,28},{40,32... | collective-permute-start | bytes 442376 | tf_op jit(solution)/shard_map/ppermute | solution.py:14
  29.0 31.1 %copy-start = (f32[1,1,3,2304]{3,1,2,0:T(1,128)S(1)}, f32[1,1,3,2304]{3,1,2,0:T(1,128)}, u32[]{:S(2)}) copy-start(f32[1,1,3,2304]{3,1,2,0:T(1,128)} %param.15) | copy-start | bytes 82948
  66.8 2.2 %copy-start.1 = (f32[256,2304]{0,1:T(8,128)S(1)}, f32[256,2304]{0,1:T(8,128)}, u32[]{:S(2)}) copy-start(f32[256,2304]{0,1:T(8,128)} %fusion.201) | copy-start | bytes 7077892 | tf_op jit(solution)/shard_map/while
  75.3 1.7 copy-start.2
  85.6 2.2 %copy-start.1 = (f32[256,2304]{0,1:T(8,128)S(1)}, f32[256,2304]{0,1:T(8,128)}, u32[]{:S(2)}) copy-start(f32[256,2304]{0,1:T(8,128)} %fusion.201) | copy-start | bytes 7077892 | tf_op jit(solution)/shard_map/while
  94.2 1.7 copy-start.2
  104.5 2.2 %copy-start.1 = (f32[256,2304]{0,1:T(8,128)S(1)}, f32[256,2304]{0,1:T(8,128)}, u32[]{:S(2)}) copy-start(f32[256,2304]{0,1:T(8,128)} %fusion.201) | copy-start | bytes 7077892 | tf_op jit(solution)/shard_map/while
  113.1 1.7 copy-start.2
  118.0 5.2 %collective-permute-start.4 = (f32[16,9,256]{2,0,1:T(8,128)S(1)}, f32[16,9,256]{2,0,1:T(8,128)S(1)}, u32[]{:S(2)}, u32[]{:S(2)}) collective-permute-start(f32[16,9,256]{2,0,1:T(8,128)S(1)} %get-tuple-element.244), channel_id=1, source_target_pairs={{8,0},{12,4},{16,8},{20,12},{24,16},{28,20},{32,24},{36,28},{40,32... | collective-permute-start | bytes 442376 | tf_op jit(solution)/shard_map/ppermute | solution.py:14
  119.8 4.2 %collective-permute-start.5 = (f32[16,9,256]{2,0,1:T(8,128)S(1)}, f32[16,9,256]{2,0,1:T(8,128)S(1)}, u32[]{:S(2)}, u32[]{:S(2)}) collective-permute-start(f32[16,9,256]{2,0,1:T(8,128)S(1)} %get-tuple-element.247), channel_id=1, source_target_pairs={{4,0},{8,4},{12,8},{16,12},{20,16},{24,20},{28,24},{32,28},{36,32}... | collective-permute-start | bytes 442376 | tf_op jit(solution)/shard_map/ppermute | solution.py:14
  119.8 7.2 %collective-permute-start.6 = (f32[16,9,256]{2,0,1:T(8,128)S(1)}, f32[16,9,256]{2,0,1:T(8,128)S(1)}, u32[]{:S(2)}, u32[]{:S(2)}) collective-permute-start(f32[16,9,256]{2,0,1:T(8,128)S(1)} %get-tuple-element.246), channel_id=1, source_target_pairs={{252,0},{0,4},{4,8},{8,12},{12,16},{16,20},{20,24},{24,28},{28,32}... | collective-permute-start | bytes 442376 | tf_op jit(solution)/shard_map/ppermute | solution.py:14
  120.3 8.8 %collective-permute-start.7 = (f32[16,9,256]{2,0,1:T(8,128)S(1)}, f32[16,9,256]{2,0,1:T(8,128)S(1)}, u32[]{:S(2)}, u32[]{:S(2)}) collective-permute-start(f32[16,9,256]{2,0,1:T(8,128)S(1)} %get-tuple-element.245), channel_id=1, source_target_pairs={{248,0},{252,4},{0,8},{4,12},{8,16},{12,20},{16,24},{20,28},{24,32... | collective-permute-start | bytes 442376 | tf_op jit(solution)/shard_map/ppermute | solution.py:14
Sparse Core Ops, SparseCore 0:
  130.0 45.3 all-reduce.1
where the time goes:
time: 184 us
  matrix products  64.5 us (35%)
  waiting for transfers between devices  55.8 us (30%)
  other arithmetic  23.4 us (13%)
  between operations  15.5 us (8%)
  local copies, waits for them, and re-layouts  13.4 us (7%)
  starting transfers between devices  10.3 us (6%)
    psum x1, waiting for transfers between devices, shards(): gauss_grad = lax.psum(block_grads, 'view')  44.9 us
    dot_general x3, matrix products, backward_task(): jnp.dot(lower_tri, log_trans, precision=precise, preferred_element_type=j...  14.8 us
    dot_general x3, matrix products, forward_task(): jnp.dot(lower_tri, log_trans, precision=precise, preferred_element_type=j...  13.9 us
    dot_general x3, matrix products, backward_task(): jnp.dot(upper_tri, weights * shaded, precision=precise, preferred_element...  13.2 us
    ppermute x8, waiting for transfers between devices, shifted(): return lax.ppermute(block, axis, route)  10.9 us
    ppermute x8, starting transfers between devices, shifted(): return lax.ppermute(block, axis, route)  10.3 us
    sub x6, other arithmetic, pixel_frame(): pix_y = (pixel_ids // TILE).astype(jnp.float32) - centre - shift[1]  7.23 us
    reduce_sum x3, other arithmetic, forward_task(): totals = jnp.sum(log_trans, axis=0)  6.89 us
  transfers between devices with their start and end apart: 9, of which 7 were waited for; matrix products, arithmetic and copies ran while one was open for 4% of the time, Pallas kernels for 0%

commit v1 on v0

--- a/solution.py
+++ b/solution.py
@@ -183,7 +183,11 @@
     for shift_by in range(-REACH, REACH + 1):
         if shift_by != 0:
             block_grads = block_grads + shifted(spread[shift_by + REACH], "cell", shift_by)
-    gauss_grad = lax.psum(block_grads, "view")
+    gauss_grad = block_grads
+    for hop in (1, 2):
+        gauss_grad = gauss_grad + lax.ppermute(
+            gauss_grad, "view", [(dev, dev ^ hop) for dev in range(4)]
+        )
     return (rendered[None, None], gauss_grad)
 
 

time: 184 us -> 143 us (0.78)
  the two profiles are of different devices: /device:TPU:8 before, /device:TPU:6 now
where the time goes in v1:
time: 143 us
  matrix products  64.5 us (45%)
  other arithmetic  25.3 us (18%)
  waiting for transfers between devices  22.3 us (16%)
  starting transfers between devices  15.9 us (11%)
  local copies, waits for them, and re-layouts  11.8 us (8%)
  between operations  2.09 us (1%)
    dot_general x3, matrix products, backward_task(): jnp.dot(lower_tri, log_trans, precision=precise, preferred_element_type=j...  14.8 us
    dot_general x3, matrix products, forward_task(): jnp.dot(lower_tri, log_trans, precision=precise, preferred_element_type=j...  13.9 us
    ppermute x8, starting transfers between devices, shifted(): return lax.ppermute(block, axis, route)  13.5 us
    dot_general x3, matrix products, backward_task(): jnp.dot(upper_tri, weights * shaded, precision=precise, preferred_element...  13.2 us
    ppermute x8, waiting for transfers between devices, shifted(): return lax.ppermute(block, axis, route)  12.4 us
    ppermute x2, waiting for transfers between devices, shards(): lax.ppermute(gauss_grad, 'view', [(dev, dev ^ hop) for dev in range(4)])  9.93 us
    sub x6, other arithmetic, pixel_frame(): pix_y = (pixel_ids // TILE).astype(jnp.float32) - centre - shift[1]  8.23 us
    reduce_sum x3, other arithmetic, forward_task(): totals = jnp.sum(log_trans, axis=0)  6.88 us
  transfers between devices with their start and end apart: 10, of which 8 were waited for; matrix products, arithmetic and copies ran while one was open for 5% of the time, Pallas kernels for 0%

profile of v1, /device:TPU:6, one launch (start us, length us, event | category | flops | bytes accessed | tf_op | source)
XLA Modules:
  0.0 142.9 jit_solution(14372255164604053403)
XLA Ops:
  0.6 1.0 copy.22
  1.6 2.0 %collective-permute-start = (f32[16,9,256]{2,1,0:T(8,128)S(1)}, f32[16,9,256]{2,1,0:T(8,128)S(1)}, u32[]{:S(2)}, u32[]{:S(2)}) collective-permute-start(f32[16,9,256]{2,1,0:T(8,128)S(1)} %copy.22), channel_id=1, source_target_pairs={{248,0},{252,4},{0,8},{4,12},{8,16},{12,20},{16,24},{20,28},{24,32... | collective-permute-start | bytes 442376 | tf_op jit(solution)/shard_map/ppermute | solution.py:14
  3.6 6.0 %collective-permute-start.2 = (f32[16,9,256]{2,1,0:T(8,128)S(1)}, f32[16,9,256]{2,1,0:T(8,128)S(1)}, u32[]{:S(2)}, u32[]{:S(2)}) collective-permute-start(f32[16,9,256]{2,1,0:T(8,128)S(1)} %copy.22), channel_id=1, source_target_pairs={{4,0},{8,4},{12,8},{16,12},{20,16},{24,20},{28,24},{32,28},{36,32}... | collective-permute-start | bytes 442376 | tf_op jit(solution)/shard_map/ppermute | solution.py:14
  9.6 2.2 %collective-permute-start.3 = (f32[16,9,256]{2,1,0:T(8,128)S(1)}, f32[16,9,256]{2,1,0:T(8,128)S(1)}, u32[]{:S(2)}, u32[]{:S(2)}) collective-permute-start(f32[16,9,256]{2,1,0:T(8,128)S(1)} %copy.22), channel_id=1, source_target_pairs={{8,0},{12,4},{16,8},{20,12},{24,16},{28,20},{32,24},{36,28},{40,32... | collective-permute-start | bytes 442376 | tf_op jit(solution)/shard_map/ppermute | solution.py:14
  11.9 0.7 fusion.126
  12.5 0.7 compare_and_fusion
  13.2 1.4 fusion.131
  16.0 1.1 collective-permute-done
  17.2 0.7 constant_dynamic-update-slice_fusion.3
  17.9 1.2 collective-permute-done.1
  19.1 0.7 constant_dynamic-update-slice_fusion.2
  19.8 1.7 %copy_dynamic-update-slice_fusion = f32[80,9,256]{2,1,0:T(8,128)} fusion(f32[80,9,256]{2,1,0:T(8,128)} %constant_dynamic-update-slice_fusion.2, f32[16,9,256]{2,0,1:T(8,128)} %param.10), kind=kLoop, calls=%fused_computation.174 | loop fusion | bytes 409600
  21.5 0.7 constant_dynamic-update-slice_fusion.1
  22.3 0.7 constant_dynamic-update-slice_fusion
  23.0 1.9 %gather_fusion = f32[3,9,256]{2,1,0:T(8,128)S(1)} fusion(f32[80,9,256]{2,1,0:T(8,128)} %constant_dynamic-update-slice_fusion, s32[1024]{0:T(1024)S(1)} %pad_clamp_fusion), kind=kCustom, calls=%fused_computation | custom fusion | bytes 55308 | tf_op jit(solution)/shard_map/jit(_take)/gather | solution.py:172
  24.9 31.3 %while.26 = (s32[]{:T(128)}, f32[3,4,2304]{2,1,0:T(4,128)S(1)}, f32[3,9,256]{2,1,0:T(8,128)S(1)}, f32[]{:T(128)}, f32[]{:T(128)}) while((s32[]{:T(128)}, f32[3,4,2304]{2,1,0:T(4,128)S(1)}, f32[3,9,256]{2,1,0:T(8,128)S(1)}, f32[]{:T(128)}, f32[]{:T(128)}) %tuple.102), condition=%wide.region_2.3_spmd.clone.clone, body=%wide.region_0.2_spmd.clone.sunk.clone | while | flops 1856945664 | bytes 4940977 | solution.py:173
  25.0 1.4 fusion.185
  26.4 4.6 %fusion.187 = f32[256,2304]{0,1:T(8,128)S(1)} fusion(f32[256]{0:T(256)S(1)} %bitcast.284, f32[256]{0:T(256)S(1)} %bitcast.276, f32[2304]{0:T(1024)S(1)} %get-tuple-element.382, f32[256]{0:T(256)S(1)} %bitcast.278, f32[256]{0:T(256)S(1)} %bitcast.280, f32[2304]{0:T(1024)S(1)} %get-tuple-element.385, f32[256]{0:T(256)S(1)} %bitcast.282, ...), kind=kOutput, calls=%fused_computation.19.clone.1.clone | convolution fusion | flops 1827405824 | bytes 2383872 | tf_op jit(solution)/shard_map/while/body/eval_jaxpr/dot_general | solution.py:45
  31.0 2.0 %fusion.188 = f32[3,2304]{1,0:T(4,128)S(1)} fusion(f32[256,2304]{0,1:T(8,128)S(1)} %fusion.187, f32[3,9,256]{2,1,0:T(8,128)S(1)} %get-tuple-element.451, s32[]{:T(128)} %get-tuple-element.444, s32[]{:T(128)S(6)} %add.588), kind=kOutput, calls=%fused_computation.48.clone.1.clone | convolution fusion | flops 21233664 | bytes 2391048 | tf_op jit(solution)/shard_map/while/body/eval_jaxpr/dot_general | solution.py:47
  33.0 2.3 %fusion.186 = f32[2304]{0:T(1024)S(1)} fusion(f32[256]{0:T(256)S(1)} %bitcast.285, f32[256]{0:T(256)S(1)} %bitcast.277, f32[2304]{0:T(1024)S(1)} %get-tuple-element.382, f32[256]{0:T(256)S(1)} %bitcast.279, f32[256]{0:T(256)S(1)} %bitcast.281, f32[2304]{0:T(1024)S(1)} %get-tuple-element.385, f32[256]{0:T(256)S(1)} %bitcast.283, f32[256]{0:T(256)S(1)} %bitcast.275), kind=kLoop, calls=%fused_computation.26.clone.1.clone | loop fusion | flops 8255232 | bytes 33792 | tf_op jit(solution)/shard_map/while/body/eval_jaxpr/reduce_sum | solution.py:48
  35.4 1.4 fusion.185
  36.8 4.6 %fusion.187 = f32[256,2304]{0,1:T(8,128)S(1)} fusion(f32[256]{0:T(256)S(1)} %bitcast.284, f32[256]{0:T(256)S(1)} %bitcast.276, f32[2304]{0:T(1024)S(1)} %get-tuple-element.382, f32[256]{0:T(256)S(1)} %bitcast.278, f32[256]{0:T(256)S(1)} %bitcast.280, f32[2304]{0:T(1024)S(1)} %get-tuple-element.385, f32[256]{0:T(256)S(1)} %bitcast.282, ...), kind=kOutput, calls=%fused_computation.19.clone.1.clone | convolution fusion | flops 1827405824 | bytes 2383872 | tf_op jit(solution)/shard_map/while/body/eval_jaxpr/dot_general | solution.py:45
  41.4 2.0 %fusion.188 = f32[3,2304]{1,0:T(4,128)S(1)} fusion(f32[256,2304]{0,1:T(8,128)S(1)} %fusion.187, f32[3,9,256]{2,1,0:T(8,128)S(1)} %get-tuple-element.451, s32[]{:T(128)} %get-tuple-element.444, s32[]{:T(128)S(6)} %add.588), kind=kOutput, calls=%fused_computation.48.clone.1.clone | convolution fusion | flops 21233664 | bytes 2391048 | tf_op jit(solution)/shard_map/while/body/eval_jaxpr/dot_general | solution.py:47
  43.4 2.3 %fusion.186 = f32[2304]{0:T(1024)S(1)} fusion(f32[256]{0:T(256)S(1)} %bitcast.285, f32[256]{0:T(256)S(1)} %bitcast.277, f32[2304]{0:T(1024)S(1)} %get-tuple-element.382, f32[256]{0:T(256)S(1)} %bitcast.279, f32[256]{0:T(256)S(1)} %bitcast.281, f32[2304]{0:T(1024)S(1)} %get-tuple-element.385, f32[256]{0:T(256)S(1)} %bitcast.283, f32[256]{0:T(256)S(1)} %bitcast.275), kind=kLoop, calls=%fused_computation.26.clone.1.clone | loop fusion | flops 8255232 | bytes 33792 | tf_op jit(solution)/shard_map/while/body/eval_jaxpr/reduce_sum | solution.py:48
  45.8 1.4 fusion.185
  47.2 4.6 %fusion.187 = f32[256,2304]{0,1:T(8,128)S(1)} fusion(f32[256]{0:T(256)S(1)} %bitcast.284, f32[256]{0:T(256)S(1)} %bitcast.276, f32[2304]{0:T(1024)S(1)} %get-tuple-element.382, f32[256]{0:T(256)S(1)} %bitcast.278, f32[256]{0:T(256)S(1)} %bitcast.280, f32[2304]{0:T(1024)S(1)} %get-tuple-element.385, f32[256]{0:T(256)S(1)} %bitcast.282, ...), kind=kOutput, calls=%fused_computation.19.clone.1.clone | convolution fusion | flops 1827405824 | bytes 2383872 | tf_op jit(solution)/shard_map/while/body/eval_jaxpr/dot_general | solution.py:45
  51.9 2.0 %fusion.188 = f32[3,2304]{1,0:T(4,128)S(1)} fusion(f32[256,2304]{0,1:T(8,128)S(1)} %fusion.187, f32[3,9,256]{2,1,0:T(8,128)S(1)} %get-tuple-element.451, s32[]{:T(128)} %get-tuple-element.444, s32[]{:T(128)S(6)} %add.588), kind=kOutput, calls=%fused_computation.48.clone.1.clone | convolution fusion | flops 21233664 | bytes 2391048 | tf_op jit(solution)/shard_map/while/body/eval_jaxpr/dot_general | solution.py:47
  53.9 2.3 %fusion.186 = f32[2304]{0:T(1024)S(1)} fusion(f32[256]{0:T(256)S(1)} %bitcast.285, f32[256]{0:T(256)S(1)} %bitcast.277, f32[2304]{0:T(1024)S(1)} %get-tuple-element.382, f32[256]{0:T(256)S(1)} %bitcast.279, f32[256]{0:T(256)S(1)} %bitcast.281, f32[2304]{0:T(1024)S(1)} %get-tuple-element.385, f32[256]{0:T(256)S(1)} %bitcast.283, f32[256]{0:T(256)S(1)} %bitcast.275), kind=kLoop, calls=%fused_computation.26.clone.1.clone | loop fusion | flops 8255232 | bytes 33792 | tf_op jit(solution)/shard_map/while/body/eval_jaxpr/reduce_sum | solution.py:48
  56.9 58.3 %while.27 = (s32[]{:T(128)}, f32[3,9,256]{2,0,1:T(4,128)S(1)}, f32[3,9,256]{2,1,0:T(8,128)S(1)}, f32[3,4,2304]{2,1,0:T(4,128)S(1)}, f32[]{:T(128)}, /*index=5*/f32[]{:T(128)}) while((s32[]{:T(128)}, f32[3,9,256]{2,0,1:T(4,128)S(1)}, f32[3,9,256]{2,1,0:T(8,128)S(1)}, f32[3,4,2304]{2,1,0:T(4,128)S(1)}, ...), condition=%wide.region_6.7_spmd.clone.clone.clone, body=%wide.region_5.6_spmd.clone.clone.sunk.clone | while | flops 3743404544 | bytes 35934480 | solution.py:177
  57.1 1.4 fusion.197
  58.5 4.9 %fusion.201 = f32[256,2304]{0,1:T(8,128)} fusion(f32[256]{0:T(256)S(1)} %bitcast.265, f32[256]{0:T(256)S(1)} %bitcast.256, f32[2304]{0:T(1024)S(1)} %get-tuple-element.410, f32[256]{0:T(256)S(1)} %bitcast.271, f32[256]{0:T(256)S(1)} %bitcast.259, f32[2304]{0:T(1024)S(1)} %get-tuple-element.409, f32[256]{0:T(256)S(1)} %bitcast.268, ...), kind=kOutput, calls=%fused_computation.66.clone.1.clone | convolution fusion | flops 1819738112 | bytes 2383872 | tf_op jit(solution)/shard_map/while/body/eval_jaxpr/dot_general | solution.py:102
  63.4 2.1 %fusion.200 = f32[256,2304]{0,1:T(8,128)S(1)} fusion(f32[3,4,2304]{2,1,0:T(4,128)S(1)} %get-tuple-element.469, s32[]{:T(128)} %get-tuple-element.460, f32[3,9,256]{2,1,0:T(8,128)S(1)} %get-tuple-element.468, s32[]{:T(128)S(6)} %add.607), kind=kOutput, calls=%fused_computation.88.clone.1.clone | convolution fusion | flops 21233664 | bytes 2401284 | tf_op jit(solution)/shard_map/while/body/eval_jaxpr/dot_general | solution.py:106
  65.6 4.4 %fusion.202 = f32[256,2304]{0,1:T(8,128)S(1)} fusion(f32[256,2304]{0,1:T(8,128)S(1)} %fusion.200, f32[256,2304]{0,1:T(8,128)S(1)} %copy-done.1, f32[2304]{0:T(1024)S(1)} %dynamic-slice_reduce_fusion.3, f32[256]{0:T(256)S(1)} %bitcast.266, f32[256]{0:T(256)S(1)} %bitcast.257, f32[2304]{0:T(1024)S(1)} %get-tuple-element.410, ...), kind=kOutput, calls=%fused_computation.70.clone.1.clone | convolution fusion | flops 1830944768 | bytes 7111680 | tf_op jit(solution)/shard_map/while/body/eval_jaxpr/dot_general | solution.py:113
  70.0 1.4 fusion.199
  71.4 0.7 fusion.198
  72.3 1.0 fusion.203
  73.9 2.2 %fusion.205 = f32[3,256]{1,0:T(4,128)S(1)} fusion(f32[256,2304]{0,1:T(8,128)S(1)} %copy-done.2, f32[256]{0:T(256)S(1)} %bitcast.267, f32[256]{0:T(256)S(1)} %bitcast.258, f32[2304]{0:T(1024)S(1)} %get-tuple-element.410, f32[256]{0:T(256)S(1)} %bitcast.273, f32[256]{0:T(256)S(1)} %bitcast.261, f32[2304]{0:T(1024)S(1)} %get-tuple-element.409, ...), kind=kOutput, calls=%fused_computation.80.clone.1.clone | convolution fusion | flops 28901376 | bytes 2429956 | tf_op jit(solution)/shard_map/while/body/eval_jaxpr/dot_general | solution.py:63
  76.4 1.4 fusion.197
  77.8 4.9 %fusion.201 = f32[256,2304]{0,1:T(8,128)} fusion(f32[256]{0:T(256)S(1)} %bitcast.265, f32[256]{0:T(256)S(1)} %bitcast.256, f32[2304]{0:T(1024)S(1)} %get-tuple-element.410, f32[256]{0:T(256)S(1)} %bitcast.271, f32[256]{0:T(256)S(1)} %bitcast.259, f32[2304]{0:T(1024)S(1)} %get-tuple-element.409, f32[256]{0:T(256)S(1)} %bitcast.268, ...), kind=kOutput, calls=%fused_computation.66.clone.1.clone | convolution fusion | flops 1819738112 | bytes 2383872 | tf_op jit(solution)/shard_map/while/body/eval_jaxpr/dot_general | solution.py:102
  82.7 2.1 %fusion.200 = f32[256,2304]{0,1:T(8,128)S(1)} fusion(f32[3,4,2304]{2,1,0:T(4,128)S(1)} %get-tuple-element.469, s32[]{:T(128)} %get-tuple-element.460, f32[3,9,256]{2,1,0:T(8,128)S(1)} %get-tuple-element.468, s32[]{:T(128)S(6)} %add.607), kind=kOutput, calls=%fused_computation.88.clone.1.clone | convolution fusion | flops 21233664 | bytes 2401284 | tf_op jit(solution)/shard_map/while/body/eval_jaxpr/dot_general | solution.py:106
  84.9 4.4 %fusion.202 = f32[256,2304]{0,1:T(8,128)S(1)} fusion(f32[256,2304]{0,1:T(8,128)S(1)} %fusion.200, f32[256,2304]{0,1:T(8,128)S(1)} %copy-done.1, f32[2304]{0:T(1024)S(1)} %dynamic-slice_reduce_fusion.3, f32[256]{0:T(256)S(1)} %bitcast.266, f32[256]{0:T(256)S(1)} %bitcast.257, f32[2304]{0:T(1024)S(1)} %get-tuple-element.410, ...), kind=kOutput, calls=%fused_computation.70.clone.1.clone | convolution fusion | flops 1830944768 | bytes 7111680 | tf_op jit(solution)/shard_map/while/body/eval_jaxpr/dot_general | solution.py:113
  89.3 1.4 fusion.199
  90.7 0.7 fusion.198
  91.6 1.0 fusion.203
  93.2 2.2 %fusion.205 = f32[3,256]{1,0:T(4,128)S(1)} fusion(f32[256,2304]{0,1:T(8,128)S(1)} %copy-done.2, f32[256]{0:T(256)S(1)} %bitcast.267, f32[256]{0:T(256)S(1)} %bitcast.258, f32[2304]{0:T(1024)S(1)} %get-tuple-element.410, f32[256]{0:T(256)S(1)} %bitcast.273, f32[256]{0:T(256)S(1)} %bitcast.261, f32[2304]{0:T(1024)S(1)} %get-tuple-element.409, ...), kind=kOutput, calls=%fused_computation.80.clone.1.clone | convolution fusion | flops 28901376 | bytes 2429956 | tf_op jit(solution)/shard_map/while/body/eval_jaxpr/dot_general | solution.py:63
  95.7 1.4 fusion.197
  97.1 4.9 %fusion.201 = f32[256,2304]{0,1:T(8,128)} fusion(f32[256]{0:T(256)S(1)} %bitcast.265, f32[256]{0:T(256)S(1)} %bitcast.256, f32[2304]{0:T(1024)S(1)} %get-tuple-element.410, f32[256]{0:T(256)S(1)} %bitcast.271, f32[256]{0:T(256)S(1)} %bitcast.259, f32[2304]{0:T(1024)S(1)} %get-tuple-element.409, f32[256]{0:T(256)S(1)} %bitcast.268, ...), kind=kOutput, calls=%fused_computation.66.clone.1.clone | convolution fusion | flops 1819738112 | bytes 2383872 | tf_op jit(solution)/shard_map/while/body/eval_jaxpr/dot_general | solution.py:102
  102.0 2.1 %fusion.200 = f32[256,2304]{0,1:T(8,128)S(1)} fusion(f32[3,4,2304]{2,1,0:T(4,128)S(1)} %get-tuple-element.469, s32[]{:T(128)} %get-tuple-element.460, f32[3,9,256]{2,1,0:T(8,128)S(1)} %get-tuple-element.468, s32[]{:T(128)S(6)} %add.607), kind=kOutput, calls=%fused_computation.88.clone.1.clone | convolution fusion | flops 21233664 | bytes 2401284 | tf_op jit(solution)/shard_map/while/body/eval_jaxpr/dot_general | solution.py:106
  104.2 4.4 %fusion.202 = f32[256,2304]{0,1:T(8,128)S(1)} fusion(f32[256,2304]{0,1:T(8,128)S(1)} %fusion.200, f32[256,2304]{0,1:T(8,128)S(1)} %copy-done.1, f32[2304]{0:T(1024)S(1)} %dynamic-slice_reduce_fusion.3, f32[256]{0:T(256)S(1)} %bitcast.266, f32[256]{0:T(256)S(1)} %bitcast.257, f32[2304]{0:T(1024)S(1)} %get-tuple-element.410, ...), kind=kOutput, calls=%fused_computation.70.clone.1.clone | convolution fusion | flops 1830944768 | bytes 7111680 | tf_op jit(solution)/shard_map/while/body/eval_jaxpr/dot_general | solution.py:113
  108.6 1.4 fusion.199
  110.0 0.7 fusion.198
  110.9 1.0 fusion.203
  112.5 2.2 %fusion.205 = f32[3,256]{1,0:T(4,128)S(1)} fusion(f32[256,2304]{0,1:T(8,128)S(1)} %copy-done.2, f32[256]{0:T(256)S(1)} %bitcast.267, f32[256]{0:T(256)S(1)} %bitcast.258, f32[2304]{0:T(1024)S(1)} %get-tuple-element.410, f32[256]{0:T(256)S(1)} %bitcast.273, f32[256]{0:T(256)S(1)} %bitcast.261, f32[2304]{0:T(1024)S(1)} %get-tuple-element.409, ...), kind=kOutput, calls=%fused_computation.80.clone.1.clone | convolution fusion | flops 28901376 | bytes 2429956 | tf_op jit(solution)/shard_map/while/body/eval_jaxpr/dot_general | solution.py:63
  115.8 2.7 %collective-permute-start.4 = (f32[16,9,256]{2,0,1:T(8,128)S(1)}, f32[16,9,256]{2,0,1:T(8,128)S(1)}, u32[]{:S(2)}, u32[]{:S(2)}) collective-permute-start(f32[16,9,256]{2,0,1:T(8,128)S(1)} %get-tuple-element.244), channel_id=1, source_target_pairs={{8,0},{12,4},{16,8},{20,12},{24,16},{28,20},{32,24},{36,28},{40,32... | collective-permute-start | bytes 442376 | tf_op jit(solution)/shard_map/ppermute | solution.py:14
  119.1 2.2 %collective-permute-done.4 = f32[16,9,256]{2,0,1:T(8,128)S(1)} collective-permute-done((f32[16,9,256]{2,0,1:T(8,128)S(1)}, f32[16,9,256]{2,0,1:T(8,128)S(1)}, u32[]{:S(2)}, u32[]{:S(2)}) %collective-permute-start.4) | collective-permute-done | bytes 147488 | tf_op jit(solution)/shard_map/ppermute | solution.py:14
  121.3 1.6 %collective-permute-done.5 = f32[16,9,256]{2,0,1:T(8,128)S(1)} collective-permute-done((f32[16,9,256]{2,0,1:T(8,128)S(1)}, f32[16,9,256]{2,0,1:T(8,128)S(1)}, u32[]{:S(2)}, u32[]{:S(2)}) %collective-permute-start.5) | collective-permute-done | bytes 147488 | tf_op jit(solution)/shard_map/ppermute | solution.py:14
  122.8 4.1 %collective-permute-done.6 = f32[16,9,256]{2,0,1:T(8,128)S(1)} collective-permute-done((f32[16,9,256]{2,0,1:T(8,128)S(1)}, f32[16,9,256]{2,0,1:T(8,128)S(1)}, u32[]{:S(2)}, u32[]{:S(2)}) %collective-permute-start.6) | collective-permute-done | bytes 147488 | tf_op jit(solution)/shard_map/ppermute | solution.py:14
  127.0 2.2 %collective-permute-done.7 = f32[16,9,256]{2,0,1:T(8,128)S(1)} collective-permute-done((f32[16,9,256]{2,0,1:T(8,128)S(1)}, f32[16,9,256]{2,0,1:T(8,128)S(1)}, u32[]{:S(2)}, u32[]{:S(2)}) %collective-permute-start.7) | collective-permute-done | bytes 147488 | tf_op jit(solution)/shard_map/ppermute | solution.py:14
  129.2 0.9 collective-permute-start.8
  130.1 5.2 %collective-permute-done.8 = f32[16,9,256]{2,0,1:T(8,128)S(1)} collective-permute-done((f32[16,9,256]{2,0,1:T(8,128)S(1)}, f32[16,9,256]{2,0,1:T(8,128)S(1)}, u32[]{:S(2)}, u32[]{:S(2)}) %collective-permute-start.8) | collective-permute-done | bytes 147488 | tf_op jit(solution)/shard_map/ppermute | solution.py:188
  135.4 1.5 %collective-permute-start.9 = (f32[16,9,256]{2,0,1:T(8,128)S(1)}, f32[16,9,256]{2,0,1:T(8,128)S(1)}, u32[]{:S(2)}, u32[]{:S(2)}) collective-permute-start(f32[16,9,256]{2,0,1:T(8,128)S(1)} %add.274), channel_id=1, source_target_pairs={{0,2},{1,3},{2,0},{3,1},{4,6},{5,7},{6,4},{7,5},{8,10},{9,11},{10,... | collective-permute-start | bytes 442376 | tf_op jit(solution)/shard_map/ppermute | solution.py:188
  136.9 0.6 reshape_multiply_fusion.1
  137.5 4.7 %collective-permute-done.9 = f32[16,9,256]{2,0,1:T(8,128)S(1)} collective-permute-done((f32[16,9,256]{2,0,1:T(8,128)S(1)}, f32[16,9,256]{2,0,1:T(8,128)S(1)}, u32[]{:S(2)}, u32[]{:S(2)}) %collective-permute-start.9) | collective-permute-done | bytes 147488 | tf_op jit(solution)/shard_map/ppermute | solution.py:188
  142.2 0.7 add.275
  (83 shorter events, 5.2 us)
Async XLA Ops:
  1.6 15.5 %collective-permute-start = (f32[16,9,256]{2,1,0:T(8,128)S(1)}, f32[16,9,256]{2,1,0:T(8,128)S(1)}, u32[]{:S(2)}, u32[]{:S(2)}) collective-permute-start(f32[16,9,256]{2,1,0:T(8,128)S(1)} %copy.22), channel_id=1, source_target_pairs={{248,0},{252,4},{0,8},{4,12},{8,16},{12,20},{16,24},{20,28},{24,32... | collective-permute-start | bytes 442376 | tf_op jit(solution)/shard_map/ppermute | solution.py:14
  3.6 15.5 %collective-permute-start.1 = (f32[16,9,256]{2,1,0:T(8,128)S(1)}, f32[16,9,256]{2,1,0:T(8,128)S(1)}, u32[]{:S(2)}, u32[]{:S(2)}) collective-permute-start(f32[16,9,256]{2,1,0:T(8,128)S(1)} %copy.22), channel_id=1, source_target_pairs={{252,0},{0,4},{4,8},{8,12},{12,16},{16,20},{20,24},{24,28},{28,32}... | collective-permute-start | bytes 442376 | tf_op jit(solution)/shard_map/ppermute | solution.py:14
  3.6 17.9 %collective-permute-start.2 = (f32[16,9,256]{2,1,0:T(8,128)S(1)}, f32[16,9,256]{2,1,0:T(8,128)S(1)}, u32[]{:S(2)}, u32[]{:S(2)}) collective-permute-start(f32[16,9,256]{2,1,0:T(8,128)S(1)} %copy.22), channel_id=1, source_target_pairs={{4,0},{8,4},{12,8},{16,12},{20,16},{24,20},{28,24},{32,28},{36,32}... | collective-permute-start | bytes 442376 | tf_op jit(solution)/shard_map/ppermute | solution.py:14
  9.6 12.6 %collective-permute-start.3 = (f32[16,9,256]{2,1,0:T(8,128)S(1)}, f32[16,9,256]{2,1,0:T(8,128)S(1)}, u32[]{:S(2)}, u32[]{:S(2)}) collective-permute-start(f32[16,9,256]{2,1,0:T(8,128)S(1)} %copy.22), channel_id=1, source_target_pairs={{8,0},{12,4},{16,8},{20,12},{24,16},{28,20},{32,24},{36,28},{40,32... | collective-permute-start | bytes 442376 | tf_op jit(solution)/shard_map/ppermute | solution.py:14
  24.9 31.6 %copy-start = (f32[1,1,3,2304]{3,1,2,0:T(1,128)S(1)}, f32[1,1,3,2304]{3,1,2,0:T(1,128)}, u32[]{:S(2)}) copy-start(f32[1,1,3,2304]{3,1,2,0:T(1,128)} %param.15) | copy-start | bytes 82948
  63.4 2.2 %copy-start.1 = (f32[256,2304]{0,1:T(8,128)S(1)}, f32[256,2304]{0,1:T(8,128)}, u32[]{:S(2)}) copy-start(f32[256,2304]{0,1:T(8,128)} %fusion.201) | copy-start | bytes 7077892 | tf_op jit(solution)/shard_map/while
  72.3 1.7 %copy-start.2 = (f32[256,2304]{0,1:T(8,128)S(1)}, f32[256,2304]{0,1:T(8,128)}, u32[]{:S(2)}) copy-start(f32[256,2304]{0,1:T(8,128)} %fusion.201) | copy-start | bytes 7077892 | tf_op jit(solution)/shard_map/while
  82.7 2.2 %copy-start.1 = (f32[256,2304]{0,1:T(8,128)S(1)}, f32[256,2304]{0,1:T(8,128)}, u32[]{:S(2)}) copy-start(f32[256,2304]{0,1:T(8,128)} %fusion.201) | copy-start | bytes 7077892 | tf_op jit(solution)/shard_map/while
  91.6 1.7 %copy-start.2 = (f32[256,2304]{0,1:T(8,128)S(1)}, f32[256,2304]{0,1:T(8,128)}, u32[]{:S(2)}) copy-start(f32[256,2304]{0,1:T(8,128)} %fusion.201) | copy-start | bytes 7077892 | tf_op jit(solution)/shard_map/while
  102.0 2.2 %copy-start.1 = (f32[256,2304]{0,1:T(8,128)S(1)}, f32[256,2304]{0,1:T(8,128)}, u32[]{:S(2)}) copy-start(f32[256,2304]{0,1:T(8,128)} %fusion.201) | copy-start | bytes 7077892 | tf_op jit(solution)/shard_map/while
  110.9 1.7 %copy-start.2 = (f32[256,2304]{0,1:T(8,128)S(1)}, f32[256,2304]{0,1:T(8,128)}, u32[]{:S(2)}) copy-start(f32[256,2304]{0,1:T(8,128)} %fusion.201) | copy-start | bytes 7077892 | tf_op jit(solution)/shard_map/while
  115.8 5.4 %collective-permute-start.4 = (f32[16,9,256]{2,0,1:T(8,128)S(1)}, f32[16,9,256]{2,0,1:T(8,128)S(1)}, u32[]{:S(2)}, u32[]{:S(2)}) collective-permute-start(f32[16,9,256]{2,0,1:T(8,128)S(1)} %get-tuple-element.244), channel_id=1, source_target_pairs={{8,0},{12,4},{16,8},{20,12},{24,16},{28,20},{32,24},{36,28},{40,32... | collective-permute-start | bytes 442376 | tf_op jit(solution)/shard_map/ppermute | solution.py:14
  118.6 4.2 %collective-permute-start.5 = (f32[16,9,256]{2,0,1:T(8,128)S(1)}, f32[16,9,256]{2,0,1:T(8,128)S(1)}, u32[]{:S(2)}, u32[]{:S(2)}) collective-permute-start(f32[16,9,256]{2,0,1:T(8,128)S(1)} %get-tuple-element.247), channel_id=1, source_target_pairs={{4,0},{8,4},{12,8},{16,12},{20,16},{24,20},{28,24},{32,28},{36,32}... | collective-permute-start | bytes 442376 | tf_op jit(solution)/shard_map/ppermute | solution.py:14
  118.6 8.4 %collective-permute-start.6 = (f32[16,9,256]{2,0,1:T(8,128)S(1)}, f32[16,9,256]{2,0,1:T(8,128)S(1)}, u32[]{:S(2)}, u32[]{:S(2)}) collective-permute-start(f32[16,9,256]{2,0,1:T(8,128)S(1)} %get-tuple-element.246), channel_id=1, source_target_pairs={{252,0},{0,4},{4,8},{8,12},{12,16},{16,20},{20,24},{24,28},{28,32}... | collective-permute-start | bytes 442376 | tf_op jit(solution)/shard_map/ppermute | solution.py:14
  119.1 10.0 %collective-permute-start.7 = (f32[16,9,256]{2,0,1:T(8,128)S(1)}, f32[16,9,256]{2,0,1:T(8,128)S(1)}, u32[]{:S(2)}, u32[]{:S(2)}) collective-permute-start(f32[16,9,256]{2,0,1:T(8,128)S(1)} %get-tuple-element.245), channel_id=1, source_target_pairs={{248,0},{252,4},{0,8},{4,12},{8,16},{12,20},{16,24},{20,28},{24,32... | collective-permute-start | bytes 442376 | tf_op jit(solution)/shard_map/ppermute | solution.py:14
  129.2 6.2 %collective-permute-start.8 = (f32[16,9,256]{2,0,1:T(8,128)S(1)}, f32[16,9,256]{2,0,1:T(8,128)S(1)}, u32[]{:S(2)}, u32[]{:S(2)}) collective-permute-start(f32[16,9,256]{2,0,1:T(8,128)S(1)} %fusion.110), channel_id=1, source_target_pairs={{0,1},{1,0},{2,3},{3,2},{4,5},{5,4},{6,7},{7,6},{8,9},{9,8},{10,11... | collective-permute-start | bytes 442376 | tf_op jit(solution)/shard_map/ppermute | solution.py:188
  135.4 6.8 %collective-permute-start.9 = (f32[16,9,256]{2,0,1:T(8,128)S(1)}, f32[16,9,256]{2,0,1:T(8,128)S(1)}, u32[]{:S(2)}, u32[]{:S(2)}) collective-permute-start(f32[16,9,256]{2,0,1:T(8,128)S(1)} %add.274), channel_id=1, source_target_pairs={{0,2},{1,3},{2,0},{3,1},{4,6},{5,7},{6,4},{7,5},{8,10},{9,11},{10,... | collective-permute-start | bytes 442376 | tf_op jit(solution)/shard_map/ppermute | solution.py:188
